TPU v7x, 32 devices: a whole 2x2x4 slice. The times are simulated.
32 devices in a mesh: row: 8 (over y, x, core), col: 4 (over z).
Axes of the slice: x: 2, y: 2, z: 4, core: 2. Of those that a mesh axis runs over, the one named last changes fastest.
Arguments:
- solution: float32 [64, 32768], P(None, ('row', 'col')), may hold values from -6 to 6
- residual: float32 [64, 65536], P(None, ('row', 'col')), may hold values from -6 to 6
- direction: float32 [64, 32768], P(None, ('row', 'col')), may hold values from -6 to 6
- jacobian_tiles: bfloat16 [512, 20, 128, 128], P('row', 'col'), may hold values from -0.125 to 0.125
- tile_blocks: int32 [512, 20], P('row', 'col'), may hold values from 0 to 63, as said below
- tile_counts: int32 [512, 4], P('row', 'col'), may hold values from 1 to 5, as said below
Outputs:
- solution_next: float32 [64, 32768], P(None, ('row', 'col'))
- residual_next: float32 [64, 65536], P(None, ('row', 'col'))
- direction_next: float32 [64, 32768], P(None, ('row', 'col'))
Inputs may be any that keep to these rules, and one draw needn't show every extreme that they name: `tile_blocks`: within each sensor and parameter group the 5 entries are different. Only the first tile_counts[i, c] slots of sensor i in group c hold a tile; some sensor fills all 5 slots of every group.
All inputs are finite; a program needn't handle non-finite values.
Results may differ from a plain program's by a relative error of at most 0.023.
Values may be sent and summed in bfloat16 or wider, within the bound.
No kernel may reach another device: no remote copies, remote signals or barrier semaphores. Data moves between devices by JAX's collectives and lax.ppermute only.
A program may use at most 128 MiB of HBM per device.

v0:
```python
import jax
import jax.numpy as jnp
from jax import lax
from jax.sharding import PartitionSpec as P

CB_DEV = 64
ITERS = 2


def times_highest(left, right):
    return jnp.dot(left, right, precision=lax.Precision.HIGHEST)


def gram_matrix(values):
    return jnp.dot(values, values.T, precision=lax.Precision.HIGHEST)


def solve_spd(matrix, right):
    factor_low = jnp.linalg.cholesky(matrix)
    middle = lax.linalg.triangular_solve(factor_low, right, left_side=True, lower=True)
    return lax.linalg.triangular_solve(
        factor_low, middle, left_side=True, lower=True, transpose_a=True
    )


def images(jacobian_tiles, tile_blocks, live_slot, direction_half):
    rhs_count = direction_half.shape[0]
    tile_width = jacobian_tiles.shape[2]
    table_view = direction_half.reshape(rhs_count, -1, tile_width)
    picked = jnp.take(table_view, tile_blocks, axis=1) * live_slot[None, :, :, None]
    product = jnp.einsum(
        "rsab,nrsb->nra", jacobian_tiles, picked, preferred_element_type=jnp.float32
    )
    return product.reshape(rhs_count, -1)


def gradients(jacobian_tiles, tile_blocks, live_slot, rows_half):
    rhs_count = rows_half.shape[0]
    tile_width = jacobian_tiles.shape[2]
    sensors = jacobian_tiles.shape[0]
    row_view = rows_half.reshape(rhs_count, sensors, tile_width)
    contrib = jnp.einsum(
        "rsab,nra->rsnb", jacobian_tiles, row_view, preferred_element_type=jnp.float32
    )
    contrib = contrib * live_slot.astype(jnp.float32)[:, :, None, None]
    summed = jax.ops.segment_sum(
        contrib.reshape(-1, rhs_count, tile_width), tile_blocks.reshape(-1), num_segments=CB_DEV
    )
    return summed.transpose(1, 0, 2).reshape(rhs_count, CB_DEV * tile_width)


def per_device(solution, residual, direction, jacobian_tiles, tile_blocks, tile_counts):
    live_slot = (
        jnp.arange(jacobian_tiles.shape[1], dtype=jnp.int32)[None, :] < tile_counts
    ).astype(jnp.bfloat16)
    share_rows = residual.shape[1]
    col_start = lax.axis_index("col") * share_rows
    rows_now = lax.all_gather(residual.astype(jnp.bfloat16), "col", axis=1, tiled=True).astype(
        residual.dtype
    )

    def gradient_step(rows_value):
        rows_half = rows_value.astype(jnp.bfloat16)
        partial_term = gradients(jacobian_tiles, tile_blocks, live_slot, rows_half)
        gradient = lax.psum_scatter(
            partial_term.astype(jnp.bfloat16), "row", scatter_dimension=1, tiled=True
        ).astype(jnp.float32)
        gamma_value = lax.psum(gram_matrix(gradient), ("row", "col"))
        return (gradient, gamma_value)

    gradient, gamma_now = gradient_step(rows_now)
    iterate = solution
    for iteration in range(ITERS):
        direction_half = lax.all_gather(direction.astype(jnp.bfloat16), "row", axis=1, tiled=True)
        image_partial_term = images(jacobian_tiles, tile_blocks, live_slot, direction_half)
        image = lax.psum(image_partial_term.astype(jnp.bfloat16), "col").astype(jnp.float32)
        curvature = lax.psum(gram_matrix(image), "row")
        image, curvature = (image, curvature)
        step_alpha = solve_spd(curvature, gamma_now)
        iterate = iterate + times_highest(step_alpha.T, direction)
        rows_now = rows_now - times_highest(step_alpha.T, image)
        gradient, gamma_next = gradient_step(rows_now)
        step_beta = solve_spd(gamma_now, gamma_next)
        direction = gradient + times_highest(step_beta.T, direction)
        gamma_now = gamma_next
    residual_out = lax.dynamic_slice_in_dim(rows_now, col_start, share_rows, 1)
    return (iterate, residual_out, direction)


def solution(mesh):
    placed = (
        P(None, ("row", "col")),
        P(None, ("row", "col")),
        P(None, ("row", "col")),
        P("row", "col", None, None),
        P("row", "col"),
        P("row", "col"),
    )
    return jax.shard_map(
        per_device,
        mesh=mesh,
        in_specs=placed,
        out_specs=(P(None, ("row", "col")), P(None, ("row", "col")), P(None, ("row", "col"))),
        check_vma=False,
    )
```

profile of v0, /device:TPU:0, one launch (start us, length us, event | category | flops | bytes accessed | tf_op | source)
XLA Modules:
  0.0 650.2 jit_solution(2488741487716216295)
XLA Ops:
  7.2 1.8 convert_element_type.98
  9.1 1.6 convert_element_type.93
  10.8 0.8 copy.50
  11.7 0.7 compare_select_fusion
  12.6 0.7 compare_and_fusion
  13.4 0.7 fusion.39
  14.2 26.7 %all-gather.6.cloned.1.call-done = bf16[64,8192]{1,0:T(8,128)(2,1)} async-done(((bf16[64,2048]{1,0:T(8,128)(2,1)}), bf16[64,8192]{1,0:T(8,128)(2,1)}) %all-gather.6.cloned.1.call-update) | async-done | bytes 1048592 | tf_op jit(solution)/shard_map/all_gather | solution.py:58
  40.9 1.5 copy.89
  42.4 10.2 %broadcast_multiply_fusion.2 = f32[64,64,5,128]{3,1,2,0:T(8,128)} fusion(f32[64,5]{1,0:T(8,128)S(1)} %get-tuple-element.8, bf16[64,5,128,128]{3,2,1,0:T(8,128)(2,1)} %param.16, bf16[64,64,128,1]{2,1,0,3:T(8,128)(2,1)S(1)} %bitcast.184), kind=kOutput, calls=%fused_computation.15 | convolution fusion | flops 673710080 | bytes 22021376 | tf_op jit(solution)/shard_map/rsab,nra->rsnb/dot_general | solution.py:42
  52.8 33.0 %scatter_fusion = f32[64,64,128]{2,1,0:T(8,128)S(1)} fusion(f32[64,64,128]{2,1,0:T(8,128)S(1)} %broadcast.76.clone, s32[320]{0:T(512)S(1)} %reshape.148, f32[320,64,128]{2,1,0:T(8,128)} %bitcast.178), kind=kCustom, calls=%fused_computation.2 | custom fusion | flops 2621440 | bytes 31458560 | tf_op jit(solution)/shard_map/scatter-add | solution.py:46
  85.8 1.5 copy_bitcast_fusion.6
  87.3 13.3 %gather_fusion = bf16[320,64,128]{2,1,0:T(8,128)(2,1)} fusion(bf16[64,64,128]{2,0,1:T(8,128)(2,1)S(1)} %copy_bitcast_fusion.6, s32[1024]{0:T(1024)S(1)} %pad_clamp_fusion), kind=kCustom, calls=%fused_computation.clone | custom fusion | bytes 10487040 | tf_op jit(solution)/shard_map/jit(_take)/gather | solution.py:30
  100.7 11.0 %fusion.10 = bf16[64,8,8,128]{3,2,1,0:T(8,128)(2,1)} fusion(bf16[64,5,128,128]{3,2,1,0:T(8,128)(2,1)} %param.16, bf16[64,5,64,128]{3,2,1,0:T(8,128)(2,1)} %bitcast.181, pred[64,5]{1,0:T(8,128)(4,1)S(1)} %copy.44, bf16[64,5]{1,0:T(8,128)(2,1)S(1)} %get-tuple-element.6), kind=kOutput, calls=%fused_computation.24 | convolution fusion | flops 676855808 | bytes 16778176 | tf_op jit(solution)/shard_map/rsab,nrsb->nra/dot_general | solution.py:31
  111.7 2.5 copy.106
  114.3 1.1 copy_bitcast_fusion.3
  116.0 49.8 %all-reduce.3.cloned.1.call-done = bf16[64,8192]{1,0:T(8,128)(2,1)} async-done(((bf16[64,8192]{1,0:T(8,128)(2,1)}), bf16[64,8192]{1,0:T(8,128)(2,1)}) %all-reduce.3.cloned.1.call-update) | async-done | bytes 1048592 | tf_op jit(solution)/shard_map/psum | solution.py:76
  165.7 2.0 fusion.44
  167.7 24.2 %psum.50 = f32[64,64]{0,1:T(8,128)S(1)} all-reduce(f32[64,64]{0,1:T(8,128)S(1)} %fusion.44), channel_id=1, replica_groups=mesh['row'=8,'col'=4] {'row'}, use_global_device_ids=true, to_apply=%region_1.3 | all-reduce | flops 4096 | bytes 32768 | tf_op jit(solution)/shard_map/psum | solution.py:77
  192.0 5.8 cholesky.74
  197.9 0.6 compare_reduce_fusion.3
  198.5 0.7 fusion.15
  199.2 4.9 custom-call.15
  204.1 1.1 fusion.45
  205.3 39.4 %psum.51 = f32[64,64]{0,1:T(8,128)S(1)} all-reduce(f32[64,64]{0,1:T(8,128)S(1)} %fusion.45), channel_id=1, replica_groups=mesh['row'=8,'col'=4] {'row','col'}, use_global_device_ids=true, to_apply=%region_6.9 | all-reduce | flops 4096 | bytes 32768 | tf_op jit(solution)/shard_map/psum | solution.py:68
  245.1 2.3 convolution_subtract_fusion.1
  247.4 1.3 copy-done
  249.2 10.2 %broadcast_multiply_fusion.1 = f32[64,64,5,128]{3,1,2,0:T(8,128)} fusion(f32[64,5]{1,0:T(8,128)S(1)} %get-tuple-element.8, bf16[64,5,128,128]{3,2,1,0:T(8,128)(2,1)} %param.16, bf16[64,64,128,1]{2,1,0,3:T(8,128)(2,1)S(1)} %bitcast.183), kind=kOutput, calls=%fused_computation.14 | convolution fusion | flops 673710080 | bytes 22021376 | tf_op jit(solution)/shard_map/rsab,nra->rsnb/dot_general | solution.py:42
  259.6 33.0 %scatter_fusion.1 = f32[64,64,128]{2,1,0:T(8,128)S(1)} fusion(f32[64,64,128]{2,1,0:T(8,128)S(1)} %broadcast.76.clone.1, s32[320]{0:T(512)S(1)} %reshape.148, f32[320,64,128]{2,1,0:T(8,128)} %bitcast.179), kind=kCustom, calls=%fused_computation.3 | custom fusion | flops 2621440 | bytes 31458560 | tf_op jit(solution)/shard_map/scatter-add | solution.py:46
  292.6 1.1 copy_bitcast_fusion.2
  293.9 5.8 cholesky.85
  299.7 0.6 compare_reduce_fusion.2
  300.4 0.7 fusion.16
  301.1 4.9 custom-call.17
  305.9 24.9 %reduce-scatter.6.cloned.1.call-done = bf16[64,1024]{1,0:T(8,128)(2,1)} async-done(((bf16[64,8192]{1,0:T(8,128)(2,1)}), bf16[64,1024]{1,0:T(8,128)(2,1)}) %reduce-scatter.6.cloned.1.call-update) | async-done | bytes 131088 | tf_op jit(solution)/shard_map/reduce_scatter | solution.py:65
  330.9 1.1 fusion.46
  332.0 39.4 %psum.52 = f32[64,64]{0,1:T(8,128)S(1)} all-reduce(f32[64,64]{0,1:T(8,128)S(1)} %fusion.46), channel_id=1, replica_groups=mesh['row'=8,'col'=4] {'row','col'}, use_global_device_ids=true, to_apply=%region_9.14 | all-reduce | flops 4096 | bytes 32768 | tf_op jit(solution)/shard_map/psum | solution.py:68
  371.9 2.0 fusion.43
  374.1 24.1 %all-gather.8.cloned.1.call-done = bf16[64,8192]{1,0:T(8,128)(2,1)} async-done(((bf16[64,1024]{1,0:T(8,128)(2,1)}), bf16[64,8192]{1,0:T(8,128)(2,1)}) %all-gather.8.cloned.1.call-update) | async-done | bytes 1048592 | tf_op jit(solution)/shard_map/all_gather | solution.py:74
  398.2 1.5 copy_bitcast_fusion.5
  399.7 13.3 %gather_fusion.1 = bf16[320,64,128]{2,1,0:T(8,128)(2,1)} fusion(bf16[64,64,128]{2,0,1:T(8,128)(2,1)S(1)} %copy_bitcast_fusion.5, s32[1024]{0:T(1024)S(1)} %pad_clamp_fusion), kind=kCustom, calls=%fused_computation.1.clone | custom fusion | bytes 10487040 | tf_op jit(solution)/shard_map/jit(_take)/gather | solution.py:30
  413.1 11.0 %fusion.11 = bf16[64,8,8,128]{3,2,1,0:T(8,128)(2,1)} fusion(bf16[64,5,128,128]{3,2,1,0:T(8,128)(2,1)} %param.16, bf16[64,5,64,128]{3,2,1,0:T(8,128)(2,1)} %bitcast.180, pred[64,5]{1,0:T(8,128)(4,1)S(1)} %copy.44, bf16[64,5]{1,0:T(8,128)(2,1)S(1)} %get-tuple-element.6), kind=kOutput, calls=%fused_computation.25 | convolution fusion | flops 676855808 | bytes 16778176 | tf_op jit(solution)/shard_map/rsab,nrsb->nra/dot_general | solution.py:31
  424.1 2.6 copy.105
  426.8 52.0 %all-reduce.5.cloned.1.call-done = bf16[64,8192]{1,0:T(8,128)(2,1)} async-done(((bf16[64,8192]{1,0:T(8,128)(2,1)}), bf16[64,8192]{1,0:T(8,128)(2,1)}) %all-reduce.5.cloned.1.call-update) | async-done | bytes 1048592 | tf_op jit(solution)/shard_map/psum | solution.py:76
  478.8 2.0 fusion.47
  480.8 24.4 %psum.54 = f32[64,64]{0,1:T(8,128)S(1)} all-reduce(f32[64,64]{0,1:T(8,128)S(1)} %fusion.47), channel_id=1, replica_groups=mesh['row'=8,'col'=4] {'row'}, use_global_device_ids=true, to_apply=%region_11.16 | all-reduce | flops 4096 | bytes 32768 | tf_op jit(solution)/shard_map/psum | solution.py:77
  505.3 5.8 cholesky.96
  511.2 0.6 compare_reduce_fusion.1
  511.8 0.7 fusion.17
  512.5 4.9 custom-call.19
  517.8 2.3 convolution_subtract_fusion
  520.1 1.3 copy-done.2
  521.9 10.2 %broadcast_multiply_fusion = f32[64,64,5,128]{3,1,2,0:T(8,128)} fusion(f32[64,5]{1,0:T(8,128)S(1)} %get-tuple-element.8, bf16[64,5,128,128]{3,2,1,0:T(8,128)(2,1)} %param.16, bf16[64,64,128,1]{2,1,0,3:T(8,128)(2,1)S(1)} %bitcast.182), kind=kOutput, calls=%fused_computation.13 | convolution fusion | flops 673710080 | bytes 22021376 | tf_op jit(solution)/shard_map/rsab,nra->rsnb/dot_general | solution.py:42
  532.3 33.0 %scatter_fusion.2 = f32[64,64,128]{2,1,0:T(8,128)S(1)} fusion(f32[64,64,128]{2,1,0:T(8,128)S(1)} %broadcast.76, s32[320]{0:T(512)S(1)} %reshape.148, f32[320,64,128]{2,1,0:T(8,128)} %bitcast.177), kind=kCustom, calls=%fused_computation.4 | custom fusion | flops 2621440 | bytes 31458560 | tf_op jit(solution)/shard_map/scatter-add | solution.py:46
  565.3 1.1 copy_bitcast_fusion
  566.9 5.8 cholesky.107
  572.8 0.6 compare_reduce_fusion
  573.5 0.7 fusion.18
  574.1 4.9 custom-call.21
  579.0 1.9 constant_dynamic-slice_fusion
  580.9 1.1 convolution_add_fusion.1
  582.0 18.1 %reduce-scatter.8.cloned.1.call-done = bf16[64,1024]{1,0:T(8,128)(2,1)} async-done(((bf16[64,8192]{1,0:T(8,128)(2,1)}), bf16[64,1024]{1,0:T(8,128)(2,1)}) %reduce-scatter.8.cloned.1.call-update) | async-done | bytes 131088 | tf_op jit(solution)/shard_map/reduce_scatter | solution.py:65
  600.1 1.1 fusion.48
  601.3 39.4 %psum.55 = f32[64,64]{1,0:T(8,128)S(1)} all-reduce(f32[64,64]{1,0:T(8,128)S(1)} %fusion.48), channel_id=1, replica_groups=mesh['row'=8,'col'=4] {'row','col'}, use_global_device_ids=true, to_apply=%region_14.19 | all-reduce | flops 4096 | bytes 32768 | tf_op jit(solution)/shard_map/psum | solution.py:68
  641.1 2.0 convolution_add_fusion
  (61 shorter events, 5.8 us)
Async XLA Ops:
  7.2 33.7 %all-gather.6.cloned.1.call-start = ((), (), s32[]{:S(2)}) async-start(), calls=%async_computation.5 | async-start | bytes 1310720 | tf_op jit(solution)/shard_map/all_gather | solution.py:58
  9.0 76.8 %all-gather.4.cloned.1.call-start = ((), (), s32[]{:S(2)}) async-start(), calls=%async_computation.3 | async-start | bytes 1179648 | tf_op jit(solution)/shard_map/all_gather | solution.py:74
  10.7 155.0 %all-reduce.3.cloned.1.call-start = ((), (), s32[]{:S(2)}) async-start(), calls=%async_computation.4 | async-start | bytes 2097152 | tf_op jit(solution)/shard_map/psum | solution.py:76
  111.7 133.4 %copy-start.3 = (bf16[64,8192]{1,0:T(8,128)(2,1)S(1)}, bf16[64,8192]{1,0:T(8,128)(2,1)}, u32[]{:S(2)}) copy-start(bf16[64,8192]{1,0:T(8,128)(2,1)} %all-gather.6.cloned.1.call-done) | copy-start | bytes 3145732
  114.3 89.9 %reduce-scatter.4.cloned.1.call-start = ((), (), s32[]{:S(2)}) async-start(), calls=%async_computation.6 | async-start | bytes 1179648 | tf_op jit(solution)/shard_map/reduce_scatter | solution.py:65
  115.4 215.4 %reduce-scatter.6.cloned.1.call-start = ((), (), s32[]{:S(2)}) async-start(), calls=%async_computation.7 | async-start | bytes 1179648 | tf_op jit(solution)/shard_map/reduce_scatter | solution.py:65
  247.4 1.3 copy-start
  259.6 112.3 %copy-start.4 = (f32[64,1024]{1,0:T(8,128)S(1)}, f32[64,1024]{1,0:T(8,128)}, u32[]{:S(2)}) copy-start(f32[64,1024]{1,0:T(8,128)} %param.15) | copy-start | bytes 786436
  293.7 104.5 %all-gather.8.cloned.1.call-start = ((), (), s32[]{:S(2)}) async-start(), calls=%async_computation.8 | async-start | bytes 1179648 | tf_op jit(solution)/shard_map/all_gather | solution.py:74
  373.9 104.9 %all-reduce.5.cloned.1.call-start = ((), (), s32[]{:S(2)}) async-start(), calls=%async_computation.9 | async-start | bytes 2097152 | tf_op jit(solution)/shard_map/psum | solution.py:76
  424.1 93.7 %copy-start.1 = (f32[64,8192]{1,0:T(8,128)S(1)}, f32[64,8192]{1,0:T(8,128)}, u32[]{:S(2)}) copy-start(f32[64,8192]{1,0:T(8,128)} %copy-done) | copy-start | bytes 6291460
  426.7 173.4 %reduce-scatter.8.cloned.1.call-start = ((), (), s32[]{:S(2)}) async-start(), calls=%async_computation.10 | async-start | bytes 1179648 | tf_op jit(solution)/shard_map/reduce_scatter | solution.py:65
  520.1 1.3 copy-start.2
  532.3 34.2 %copy-start.5 = (f32[64,1024]{1,0:T(8,128)S(1)}, f32[64,1024]{1,0:T(8,128)}, u32[]{:S(2)}) copy-start(f32[64,1024]{1,0:T(8,128)} %param.13) | copy-start | bytes 786436
Sparse Core Ops, SparseCore 0:
  10.1 30.6 all-gather.5
  43.3 22.7 all-gather.3
  114.4 51.2 all-reduce.2
  168.7 35.3 reduce-scatter.3
  293.8 36.9 reduce-scatter.5
  374.0 24.1 all-gather.7
  426.9 51.8 all-reduce.4
  566.5 33.5 reduce-scatter.7
where the time goes:
time: 662 us; the launch traced here: 650 us
  waiting for transfers between devices  196 us (30%)
  blocking collectives  167 us (25%)
  other arithmetic  156 us (24%)
  matrix products  71.7 us (11%)
  local copies, waits for them, and re-layouts  43.6 us (7%)
  between operations  14.8 us (2%)
    psum x3, blocking collectives, gradient_step(): gamma_value = lax.psum(gram_matrix(gradient), ('row', 'col'))  118 us
    psum x2, waiting for transfers between devices, per_device(): lax.psum(image_partial_term.astype(jnp.bfloat16), 'col').astype(jnp.float32)  102 us
    scatter-add x3, other arithmetic, gradients(): jax.ops.segment_sum(contrib.reshape(-1, rhs_count, tile_width), tile_bloc...  99 us
    psum x2, blocking collectives, per_device(): curvature = lax.psum(gram_matrix(image), 'row')  48.6 us
    reduce_scatter x3, waiting for transfers between devices, gradient_step(): lax.psum_scatter(partial_term.astype(jnp.bfloat16), 'row', scatter_dimens...  43.1 us
    dot_general x3, matrix products, gradients(): jnp.einsum('rsab,nra->rsnb', jacobian_tiles, row_view, preferred_element_...  30.5 us
    all_gather x1, waiting for transfers between devices, per_device(): lax.all_gather(residual.astype(jnp.bfloat16), 'col', axis=1, tiled=True)  26.7 us
    gather x2, local copies, waits for them, and re-layouts, images(): jnp.take(table_view, tile_blocks, axis=1) * live_slot[None, :, :, None]  26.7 us
  transfers between devices with their start and end apart: 8, of which 7 were waited for; matrix products, arithmetic and copies ran while one was open for 14% of the time, Pallas kernels for 0%

commit v1 on v0

--- a/solution.py
+++ b/solution.py
@@ -65,7 +65,9 @@
         gradient = lax.psum_scatter(
             partial_term.astype(jnp.bfloat16), "row", scatter_dimension=1, tiled=True
         ).astype(jnp.float32)
-        gamma_value = lax.psum(gram_matrix(gradient), ("row", "col"))
+        part = gram_matrix(gradient)
+        parts = lax.all_gather(part, ("row", "col"))
+        gamma_value = jnp.sum(parts, axis=0)
         return (gradient, gamma_value)
 
     gradient, gamma_now = gradient_step(rows_now)

time: 662 us -> 762 us (1.15)
  blocking collectives: 167 us -> 277 us
    all_gather x0 -> x3, blocking collectives: none -> 229 us  [gradient_step(): parts = lax.all_gather(part, ('row', 'col'))]
    psum x3 -> x0, blocking collectives: 118 us -> none  [gradient_step(): gamma_value = lax.psum(gram_matrix(gradient), ('row', 'col'))]
  transfers between devices with their start and end apart: 8 -> 8, of which waited for: 7 -> 6; matrix products, arithmetic and copies ran while one was open for 14% -> 12% of each run, Pallas kernels for 0% -> 0%
where the time goes in v1:
time: 762 us; the launch traced here: 750 us
  blocking collectives  277 us (36%)
  waiting for transfers between devices  189 us (25%)
  other arithmetic  157 us (21%)
  matrix products  69.5 us (9%)
  local copies, waits for them, and re-layouts  42.3 us (6%)
  between operations  14.8 us (2%)
    all_gather x3, blocking collectives, gradient_step(): parts = lax.all_gather(part, ('row', 'col'))  229 us
    psum x2, waiting for transfers between devices, per_device(): lax.psum(image_partial_term.astype(jnp.bfloat16), 'col').astype(jnp.float32)  102 us
    scatter-add x3, other arithmetic, gradients(): jax.ops.segment_sum(contrib.reshape(-1, rhs_count, tile_width), tile_bloc...  99 us
    psum x2, blocking collectives, per_device(): curvature = lax.psum(gram_matrix(image), 'row')  48.6 us
    reduce_scatter x3, waiting for transfers between devices, gradient_step(): lax.psum_scatter(partial_term.astype(jnp.bfloat16), 'row', scatter_dimens...  39.5 us
    dot_general x3, matrix products, gradients(): jnp.einsum('rsab,nra->rsnb', jacobian_tiles, row_view, preferred_element_...  30.5 us
    all_gather x1, waiting for transfers between devices, per_device(): lax.all_gather(residual.astype(jnp.bfloat16), 'col', axis=1, tiled=True)  26.7 us
    gather x2, local copies, waits for them, and re-layouts, images(): jnp.take(table_view, tile_blocks, axis=1) * live_slot[None, :, :, None]  26.7 us
  transfers between devices with their start and end apart: 8, of which 6 were waited for; matrix products, arithmetic and copies ran while one was open for 12% of the time, Pallas kernels for 0%

profile of v1, /device:TPU:0, one launch (start us, length us, event | category | flops | bytes accessed | tf_op | source)
XLA Modules:
  0.0 750.3 jit_solution(7412588432575185843)
XLA Ops:
  7.2 1.8 convert_element_type.98
  9.1 1.6 convert_element_type.93
  10.8 0.8 copy.67
  11.7 0.7 compare_select_fusion
  12.6 0.7 compare_and_fusion
  13.4 0.7 fusion.39
  14.2 26.7 %all-gather.9.cloned.1.call-done = bf16[64,8192]{1,0:T(8,128)(2,1)} async-done(((bf16[64,2048]{1,0:T(8,128)(2,1)}), bf16[64,8192]{1,0:T(8,128)(2,1)}) %all-gather.9.cloned.1.call-update) | async-done | bytes 1048592 | tf_op jit(solution)/shard_map/all_gather | solution.py:58
  40.9 1.5 copy.102
  42.4 10.2 %broadcast_multiply_fusion.2 = f32[64,64,5,128]{3,1,2,0:T(8,128)} fusion(f32[64,5]{1,0:T(8,128)S(1)} %get-tuple-element.8, bf16[64,5,128,128]{3,2,1,0:T(8,128)(2,1)} %param.16, bf16[64,64,128,1]{2,1,0,3:T(8,128)(2,1)S(1)} %bitcast.187), kind=kOutput, calls=%fused_computation.15 | convolution fusion | flops 673710080 | bytes 22021376 | tf_op jit(solution)/shard_map/rsab,nra->rsnb/dot_general | solution.py:42
  52.8 33.0 %scatter_fusion = f32[64,64,128]{2,1,0:T(8,128)S(1)} fusion(f32[64,64,128]{2,1,0:T(8,128)S(1)} %broadcast.76.clone, s32[320]{0:T(512)S(1)} %reshape.148, f32[320,64,128]{2,1,0:T(8,128)} %bitcast.181), kind=kCustom, calls=%fused_computation.2 | custom fusion | flops 2621440 | bytes 31458560 | tf_op jit(solution)/shard_map/scatter-add | solution.py:46
  85.8 1.5 copy_bitcast_fusion.6
  87.3 13.3 %gather_fusion = bf16[320,64,128]{2,1,0:T(8,128)(2,1)} fusion(bf16[64,64,128]{2,0,1:T(8,128)(2,1)S(1)} %copy_bitcast_fusion.6, s32[1024]{0:T(1024)S(1)} %pad_clamp_fusion), kind=kCustom, calls=%fused_computation.clone | custom fusion | bytes 10487040 | tf_op jit(solution)/shard_map/jit(_take)/gather | solution.py:30
  100.7 10.0 %fusion.10 = bf16[64,8,8,128]{3,2,1,0:T(8,128)(2,1)S(1)} fusion(bf16[64,5,128,128]{3,2,1,0:T(8,128)(2,1)} %param.16, bf16[64,5,64,128]{3,2,1,0:T(8,128)(2,1)} %bitcast.184, pred[64,5]{1,0:T(8,128)(4,1)S(1)} %copy.61, bf16[64,5]{1,0:T(8,128)(2,1)S(1)} %get-tuple-element.6), kind=kOutput, calls=%fused_computation.24 | convolution fusion | flops 676855808 | bytes 16778176 | tf_op jit(solution)/shard_map/rsab,nrsb->nra/dot_general | solution.py:31
  110.7 1.2 copy.119
  112.0 1.1 copy_bitcast_fusion.3
  113.6 49.8 %all-reduce.3.cloned.1.call-done = bf16[64,8192]{1,0:T(8,128)(2,1)} async-done(((bf16[64,8192]{1,0:T(8,128)(2,1)}), bf16[64,8192]{1,0:T(8,128)(2,1)}) %all-reduce.3.cloned.1.call-update) | async-done | bytes 1048592 | tf_op jit(solution)/shard_map/psum | solution.py:78
  163.4 2.0 fusion.44
  165.4 24.2 %psum.29 = f32[64,64]{0,1:T(8,128)S(1)} all-reduce(f32[64,64]{0,1:T(8,128)S(1)} %fusion.44), channel_id=1, replica_groups=mesh['row'=8,'col'=4] {'row'}, use_global_device_ids=true, to_apply=%region_1.3 | all-reduce | flops 4096 | bytes 32768 | tf_op jit(solution)/shard_map/psum | solution.py:79
  189.7 5.8 cholesky.74
  195.6 0.6 compare_reduce_fusion.3
  196.3 0.7 fusion.15
  196.9 4.9 custom-call.15
  201.9 1.1 fusion.45
  203.0 76.0 %all-gather = f32[2048,64]{1,0:T(8,128)S(1)} all-gather(f32[64,64]{1,0:T(8,128)S(1)} %fusion.45), channel_id=2, replica_groups=mesh['row'=8,'col'=4] {'row','col'}, dimensions={0}, use_global_device_ids=true | all-gather | bytes 540672 | tf_op jit(solution)/shard_map/all_gather | solution.py:69
  279.5 1.1 convolution_subtract_fusion.1
  280.6 1.3 copy-done
  282.4 10.2 %broadcast_multiply_fusion.1 = f32[64,64,5,128]{3,1,2,0:T(8,128)} fusion(f32[64,5]{1,0:T(8,128)S(1)} %get-tuple-element.8, bf16[64,5,128,128]{3,2,1,0:T(8,128)(2,1)} %param.16, bf16[64,64,128,1]{2,1,0,3:T(8,128)(2,1)S(1)} %bitcast.186), kind=kOutput, calls=%fused_computation.14 | convolution fusion | flops 673710080 | bytes 22021376 | tf_op jit(solution)/shard_map/rsab,nra->rsnb/dot_general | solution.py:42
  292.8 33.0 %scatter_fusion.1 = f32[64,64,128]{2,1,0:T(8,128)S(1)} fusion(f32[64,64,128]{2,1,0:T(8,128)S(1)} %broadcast.76.clone.1, s32[320]{0:T(512)S(1)} %reshape.148, f32[320,64,128]{2,1,0:T(8,128)} %bitcast.182), kind=kCustom, calls=%fused_computation.3 | custom fusion | flops 2621440 | bytes 31458560 | tf_op jit(solution)/shard_map/scatter-add | solution.py:46
  325.8 1.1 copy_bitcast_fusion.2
  327.1 5.8 cholesky.85
  332.9 0.6 compare_reduce_fusion.2
  333.6 0.7 fusion.16
  334.2 4.9 custom-call.17
  339.1 21.5 %reduce-scatter.6.cloned.1.call-done = bf16[64,1024]{1,0:T(8,128)(2,1)} async-done(((bf16[64,8192]{1,0:T(8,128)(2,1)}), bf16[64,1024]{1,0:T(8,128)(2,1)}) %reduce-scatter.6.cloned.1.call-update) | async-done | bytes 131088 | tf_op jit(solution)/shard_map/reduce_scatter | solution.py:65
  360.6 1.1 fusion.46
  361.8 76.1 %all-gather.1 = f32[2048,64]{1,0:T(8,128)S(1)} all-gather(f32[64,64]{1,0:T(8,128)S(1)} %fusion.46), channel_id=3, replica_groups=mesh['row'=8,'col'=4] {'row','col'}, dimensions={0}, use_global_device_ids=true | all-gather | bytes 540672 | tf_op jit(solution)/shard_map/all_gather | solution.py:69
  438.4 2.0 fusion.43
  440.6 20.6 %all-gather.11.cloned.1.call-done = bf16[64,8192]{1,0:T(8,128)(2,1)} async-done(((bf16[64,1024]{1,0:T(8,128)(2,1)}), bf16[64,8192]{1,0:T(8,128)(2,1)}) %all-gather.11.cloned.1.call-update) | async-done | bytes 1048592 | tf_op jit(solution)/shard_map/all_gather | solution.py:76
  461.2 1.5 copy_bitcast_fusion.5
  462.7 13.3 %gather_fusion.1 = bf16[320,64,128]{2,1,0:T(8,128)(2,1)} fusion(bf16[64,64,128]{2,0,1:T(8,128)(2,1)S(1)} %copy_bitcast_fusion.5, s32[1024]{0:T(1024)S(1)} %pad_clamp_fusion), kind=kCustom, calls=%fused_computation.1.clone | custom fusion | bytes 10487040 | tf_op jit(solution)/shard_map/jit(_take)/gather | solution.py:30
  476.1 11.0 %fusion.11 = bf16[64,8,8,128]{3,2,1,0:T(8,128)(2,1)} fusion(bf16[64,5,128,128]{3,2,1,0:T(8,128)(2,1)} %param.16, bf16[64,5,64,128]{3,2,1,0:T(8,128)(2,1)} %bitcast.183, pred[64,5]{1,0:T(8,128)(4,1)S(1)} %copy.61, bf16[64,5]{1,0:T(8,128)(2,1)S(1)} %get-tuple-element.6), kind=kOutput, calls=%fused_computation.25 | convolution fusion | flops 676855808 | bytes 16778176 | tf_op jit(solution)/shard_map/rsab,nrsb->nra/dot_general | solution.py:31
  487.1 2.6 copy.118
  489.8 52.0 %all-reduce.5.cloned.1.call-done = bf16[64,8192]{1,0:T(8,128)(2,1)} async-done(((bf16[64,8192]{1,0:T(8,128)(2,1)}), bf16[64,8192]{1,0:T(8,128)(2,1)}) %all-reduce.5.cloned.1.call-update) | async-done | bytes 1048592 | tf_op jit(solution)/shard_map/psum | solution.py:78
  541.8 2.0 fusion.47
  543.8 24.4 %psum.31 = f32[64,64]{0,1:T(8,128)S(1)} all-reduce(f32[64,64]{0,1:T(8,128)S(1)} %fusion.47), channel_id=1, replica_groups=mesh['row'=8,'col'=4] {'row'}, use_global_device_ids=true, to_apply=%region_11.16 | all-reduce | flops 4096 | bytes 32768 | tf_op jit(solution)/shard_map/psum | solution.py:79
  568.3 5.8 cholesky.96
  574.2 0.6 compare_reduce_fusion.1
  574.8 0.7 fusion.17
  575.5 4.9 custom-call.19
  580.8 2.3 convolution_subtract_fusion
  583.1 1.3 copy-done.2
  584.9 10.2 %broadcast_multiply_fusion = f32[64,64,5,128]{3,1,2,0:T(8,128)} fusion(f32[64,5]{1,0:T(8,128)S(1)} %get-tuple-element.8, bf16[64,5,128,128]{3,2,1,0:T(8,128)(2,1)} %param.16, bf16[64,64,128,1]{2,1,0,3:T(8,128)(2,1)S(1)} %bitcast.185), kind=kOutput, calls=%fused_computation.13 | convolution fusion | flops 673710080 | bytes 22021376 | tf_op jit(solution)/shard_map/rsab,nra->rsnb/dot_general | solution.py:42
  595.3 33.0 %scatter_fusion.2 = f32[64,64,128]{2,1,0:T(8,128)S(1)} fusion(f32[64,64,128]{2,1,0:T(8,128)S(1)} %broadcast.76, s32[320]{0:T(512)S(1)} %reshape.148, f32[320,64,128]{2,1,0:T(8,128)} %bitcast.180), kind=kCustom, calls=%fused_computation.4 | custom fusion | flops 2621440 | bytes 31458560 | tf_op jit(solution)/shard_map/scatter-add | solution.py:46
  628.3 1.1 copy_bitcast_fusion
  630.0 5.8 cholesky.107
  635.8 0.6 compare_reduce_fusion
  636.5 0.7 fusion.18
  637.1 4.9 custom-call.21
  642.0 1.9 constant_dynamic-slice_fusion
  643.9 1.1 convolution_add_fusion.1
  645.0 18.0 %reduce-scatter.8.cloned.1.call-done = bf16[64,1024]{1,0:T(8,128)(2,1)} async-done(((bf16[64,8192]{1,0:T(8,128)(2,1)}), bf16[64,1024]{1,0:T(8,128)(2,1)}) %reduce-scatter.8.cloned.1.call-update) | async-done | bytes 131088 | tf_op jit(solution)/shard_map/reduce_scatter | solution.py:65
  663.1 1.1 fusion.48
  664.2 76.5 %all-gather.2 = f32[2048,64]{1,0:T(8,128)S(1)} all-gather(f32[64,64]{1,0:T(8,128)S(1)} %fusion.48), channel_id=4, replica_groups=mesh['row'=8,'col'=4] {'row','col'}, dimensions={0}, use_global_device_ids=true | all-gather | bytes 540672 | tf_op jit(solution)/shard_map/all_gather | solution.py:69
  741.2 2.0 convolution_add_fusion
  (66 shorter events, 6.0 us)
Async XLA Ops:
  7.2 33.7 %all-gather.9.cloned.1.call-start = ((), (), s32[]{:S(2)}) async-start(), calls=%async_computation.5 | async-start | bytes 1310720 | tf_op jit(solution)/shard_map/all_gather | solution.py:58
  9.0 76.8 %all-gather.7.cloned.1.call-start = ((), (), s32[]{:S(2)}) async-start(), calls=%async_computation.3 | async-start | bytes 1179648 | tf_op jit(solution)/shard_map/all_gather | solution.py:76
  10.7 152.7 %all-reduce.3.cloned.1.call-start = ((), (), s32[]{:S(2)}) async-start(), calls=%async_computation.4 | async-start | bytes 2097152 | tf_op jit(solution)/shard_map/psum | solution.py:78
  111.9 167.6 %copy-start.4 = (bf16[64,8192]{1,0:T(8,128)(2,1)S(1)}, bf16[64,8192]{1,0:T(8,128)(2,1)}, u32[]{:S(2)}) copy-start(bf16[64,8192]{1,0:T(8,128)(2,1)} %all-gather.9.cloned.1.call-done) | copy-start | bytes 3145732
  111.9 89.9 %reduce-scatter.4.cloned.1.call-start = ((), (), s32[]{:S(2)}) async-start(), calls=%async_computation.6 | async-start | bytes 1179648 | tf_op jit(solution)/shard_map/reduce_scatter | solution.py:65
  113.1 247.5 %reduce-scatter.6.cloned.1.call-start = ((), (), s32[]{:S(2)}) async-start(), calls=%async_computation.7 | async-start | bytes 1179648 | tf_op jit(solution)/shard_map/reduce_scatter | solution.py:65
  163.4 116.1 %copy-start.3 = (bf16[64,8192]{1,0:T(8,128)(2,1)S(1)}, bf16[64,8192]{1,0:T(8,128)(2,1)}, u32[]{:S(2)}) copy-start(bf16[64,8192]{1,0:T(8,128)(2,1)} %all-reduce.3.cloned.1.call-done) | copy-start | bytes 3145732
  280.6 1.3 copy-start
  325.8 112.6 %copy-start.5 = (f32[64,1024]{1,0:T(8,128)S(1)}, f32[64,1024]{1,0:T(8,128)}, u32[]{:S(2)}) copy-start(f32[64,1024]{1,0:T(8,128)} %param.15) | copy-start | bytes 786436
  326.9 134.3 %all-gather.11.cloned.1.call-start = ((), (), s32[]{:S(2)}) async-start(), calls=%async_computation.8 | async-start | bytes 1179648 | tf_op jit(solution)/shard_map/all_gather | solution.py:76
  440.4 101.4 %all-reduce.5.cloned.1.call-start = ((), (), s32[]{:S(2)}) async-start(), calls=%async_computation.9 | async-start | bytes 2097152 | tf_op jit(solution)/shard_map/psum | solution.py:78
  487.1 93.7 %copy-start.1 = (f32[64,8192]{1,0:T(8,128)S(1)}, f32[64,8192]{1,0:T(8,128)}, u32[]{:S(2)}) copy-start(f32[64,8192]{1,0:T(8,128)} %copy-done) | copy-start | bytes 6291460
  489.7 173.3 %reduce-scatter.8.cloned.1.call-start = ((), (), s32[]{:S(2)}) async-start(), calls=%async_computation.10 | async-start | bytes 1179648 | tf_op jit(solution)/shard_map/reduce_scatter | solution.py:65
  583.1 1.3 copy-start.2
  595.3 34.2 %copy-start.6 = (f32[64,1024]{1,0:T(8,128)S(1)}, f32[64,1024]{1,0:T(8,128)}, u32[]{:S(2)}) copy-start(f32[64,1024]{1,0:T(8,128)} %param.13) | copy-start | bytes 786436
Sparse Core Ops, SparseCore 0:
  10.1 30.6 all-gather.8
  43.3 22.7 all-gather.6
  112.1 51.2 all-reduce.2
  166.4 35.3 reduce-scatter.3
  327.0 33.5 reduce-scatter.5
  440.5 20.6 all-gather.10
  489.9 51.8 all-reduce.4
  629.5 33.4 reduce-scatter.7
